TPU v7x, 32 devices: a whole 2x2x4 slice. The times are simulated.
32 devices in a mesh: pop: 16 (over z, x, core), tp: 2 (over y).
Axes of the slice: x: 2, y: 2, z: 4, core: 2. Of those that a mesh axis runs over, the one named last changes fastest.
Arguments:
- tokens: bfloat16 [6144, 3584], P(('pop', 'tp')), may hold values from -6 to 6
- norm_gain: bfloat16 [3584], replicated, may hold values from 0.5 to 1.5
- weight: bfloat16 [3584, 10240], P('pop', 'tp'), may hold values from -0.09375 to 0.09375
- pair_seeds: int32 [32], P('pop'), may hold values from 0 to 1073741823
- member_ranks: int32 [64], P('pop'), may hold values from 0 to 63, each once
Outputs:
- activated: bfloat16 [6144, 10240], P('pop', 'tp')
- estimate: float32 [3584, 10240], P('pop', 'tp')
Inputs may be any that keep to these rules, and one draw needn't show every extreme that they name: `member_ranks`: each of 0 to 63 appears once.
All inputs are finite; a program needn't handle non-finite values.
Results may differ from a plain program's by a relative error of at most 0.0051.
Values may be sent and summed in bfloat16 or wider, within the bound.
A program may use at most 128 MiB of HBM per device.

v0:
```python
import math

import jax
import jax.numpy as jnp
from jax import lax
from jax.sharding import PartitionSpec as P

FFW = 10240
ROWS = 96


noise_scale = 0.01
mix_seed = -1640531535
mix_first = -2048144789
mix_second = -1028477387


def shifted(values, amount):
    return lax.shift_right_logical(values, jnp.full_like(values, amount))


def noise_block(seed_value, row_ids, col_ids):
    counter = row_ids[:, None] * jnp.int32(FFW) + col_ids[None, :]
    hashed = seed_value * jnp.int32(mix_seed) + counter
    hashed = hashed ^ shifted(hashed, 16)
    hashed = hashed * jnp.int32(mix_first)
    hashed = hashed ^ shifted(hashed, 13)
    hashed = hashed * jnp.int32(mix_second)
    hashed = hashed ^ shifted(hashed, 16)
    lower = hashed & 255
    upper = shifted(hashed, 8) & 255
    return (lower + upper - 255).astype(jnp.float32) / 128.0


def normalize(tokens, norm_gain):
    values = tokens.astype(jnp.float32)
    factor = lax.rsqrt(jnp.mean(values * values, axis=1, keepdims=True) + 1e-06)
    return (values * factor * norm_gain.astype(jnp.float32)).astype(jnp.bfloat16)


def make_fold(normed, seed_list, col_ids, segment, offset):
    pair_count = seed_list.shape[0]
    span_rows = normed.shape[0] // pair_count
    length = segment.shape[0]
    base_sum = jnp.dot(normed, segment, preferred_element_type=jnp.float32)
    pieces = []
    for pair_index in range(pair_count):
        pair_rows = normed[pair_index * span_rows : (pair_index + 1) * span_rows]
        partial_value = jnp.zeros((span_rows, col_ids.shape[0]), jnp.float32)
        for lower_row in range(0, length, 512):
            height = min(512, length - lower_row)
            row_ids = offset + lower_row + jnp.arange(height, dtype=jnp.int32)
            sample = noise_block(seed_list[pair_index], row_ids, col_ids).astype(jnp.bfloat16)
            partial_value = partial_value + jnp.dot(
                pair_rows[:, lower_row : lower_row + height],
                sample,
                preferred_element_type=jnp.float32,
            )
        pieces.append(partial_value)
    return (base_sum, jnp.concatenate(pieces, 0))


def activate(base_sum, noise_sum):
    member_count = base_sum.shape[0] // ROWS
    pattern = jnp.repeat(jnp.array([1.0, -1.0], jnp.float32), ROWS)
    signed = jnp.tile(pattern, member_count // 2)[:, None]
    return jax.nn.silu(base_sum + noise_scale * signed * noise_sum).astype(jnp.bfloat16)


def shards(tokens, norm_gain, weight, pair_seeds, member_ranks):
    all_seeds, all_ranks = (
        lax.all_gather(pair_seeds, "pop", axis=0, tiled=True),
        lax.all_gather(member_ranks, "pop", axis=0, tiled=True),
    )
    gathered = lax.all_gather(tokens, "tp", axis=0, tiled=True)
    normed = normalize(gathered, norm_gain)
    owned_rows = weight.shape[0]
    width = weight.shape[1]
    pop_index = lax.axis_index("pop")
    col_start = lax.axis_index("tp") * width
    col_ids = col_start + jnp.arange(width, dtype=jnp.int32)
    base_sum, noise_sum = make_fold(
        normed, pair_seeds, col_ids, lax.all_gather(weight, "pop", axis=0, tiled=True), jnp.int32(0)
    )
    activated = activate(base_sum, noise_sum)
    members = all_ranks.shape[0]
    coefs = (all_ranks[0::2] - all_ranks[1::2]).astype(jnp.float32) / (
        (members - 1) * members * noise_scale
    )
    group_size = math.gcd(16, all_seeds.shape[0])
    row_ids = pop_index * owned_rows + jnp.arange(owned_rows, dtype=jnp.int32)
    owned_cols = col_start + jnp.arange(width, dtype=jnp.int32)

    def accumulate(running, bundle):
        group_seeds, group_coefs = bundle
        samples = jax.vmap(lambda one_seed: noise_block(one_seed, row_ids, owned_cols))(group_seeds)
        return (running + jnp.sum(group_coefs[:, None, None] * samples, axis=0), None)

    estimate, unused_out = lax.scan(
        accumulate,
        jnp.zeros((owned_rows, width), jnp.float32),
        (all_seeds.reshape(-1, group_size), coefs.reshape(-1, group_size)),
    )
    return (activated, estimate)


def solution(mesh):
    placed = (P(("pop", "tp"), None), P(), P("pop", "tp"), P("pop"), P("pop"))
    return jax.shard_map(
        shards,
        mesh=mesh,
        in_specs=placed,
        out_specs=(P("pop", "tp"), P("pop", "tp")),
        check_vma=False,
    )
```

profile of v0, /device:TPU:0, one launch (start us, length us, event | category | flops | bytes accessed | tf_op | source)
XLA Modules:
  0.0 270.1 jit_solution(3130930715908840641)
XLA Ops:
  12.9 13.7 %all-reduce.2 = (s32[32]{0:T(128)S(1)}, s32[64]{0:T(128)S(1)}) all-reduce(s32[32]{0:T(128)S(1)} %dynamic-update-slice, s32[64]{0:T(128)S(1)} %dynamic-update-slice.1), channel_id=1, replica_groups=mesh['pop'=16,'tp'=2] {'pop'}, use_global_device_ids=true, to_apply=%add | all-reduce | flops 96 | bytes 768
  27.6 1.3 fusion.320
  33.0 102.9 %while.13 = (s32[]{:T(128)}, f32[224,5120]{1,0:T(8,128)}, s32[2,16]{1,0:T(2,128)S(1)}, f32[2,16]{1,0:T(2,128)S(1)}, s32[]{:T(128)}, /*index=5*/s32[]{:T(128)}, s32[]{:T(128)}, s32[]{:T(128)}) while((s32[]{:T(128)}, f32[224,5120]{1,0:T(8,128)}, s32[2,16]{1,0:T(2,128)S(1)}, f32[2,16]{1,0:T(2,128)S(1)}, s32[]{:T(128)}, ...), condition=%wide.region_3.4_spmd.clone, body=%wide.region_1.3_spmd.clone.sunk | while | flops 314250720 | bytes 27568368 | solution.py:99
  33.6 44.7 %multiply_reduce_fusion.2 = f32[224,5120]{1,0:T(8,128)} fusion(f32[16]{0:T(128)S(1)} %multiply_bitcast_fusion.4, s32[224,5120]{1,0:T(8,128)S(1)} %broadcast_add_fusion.2, s32[16]{0:T(128)S(1)} %multiply_bitcast_fusion.5), kind=kLoop, calls=%fused_computation.7.clone.1 | loop fusion | flops 310804480 | bytes 9175168 | tf_op jit(solution)/shard_map/while/body/eval_jaxpr/reduce_sum | solution.py:97
  78.3 5.2 %select_add_fusion.2 = f32[224,5120]{1,0:T(8,128)} fusion(f32[224,5120]{1,0:T(8,128)} %multiply_reduce_fusion.2, f32[224,5120]{1,0:T(8,128)} %get-tuple-element.169, pred[]{:T(512)S(6)} %compare.3), kind=kLoop, calls=%fused_computation.8.clone.1 | loop fusion | flops 2293760 | bytes 13762561 | tf_op jit(solution)/shard_map/while/body/eval_jaxpr/add | solution.py:97
  84.1 44.7 %multiply_reduce_fusion.2 = f32[224,5120]{1,0:T(8,128)} fusion(f32[16]{0:T(128)S(1)} %multiply_bitcast_fusion.4, s32[224,5120]{1,0:T(8,128)S(1)} %broadcast_add_fusion.2, s32[16]{0:T(128)S(1)} %multiply_bitcast_fusion.5), kind=kLoop, calls=%fused_computation.7.clone.1 | loop fusion | flops 310804480 | bytes 9175168 | tf_op jit(solution)/shard_map/while/body/eval_jaxpr/reduce_sum | solution.py:97
  128.9 6.8 %select_add_fusion.2 = f32[224,5120]{1,0:T(8,128)} fusion(f32[224,5120]{1,0:T(8,128)} %multiply_reduce_fusion.2, f32[224,5120]{1,0:T(8,128)} %get-tuple-element.169, pred[]{:T(512)S(6)} %compare.3), kind=kLoop, calls=%fused_computation.8.clone.1 | loop fusion | flops 2293760 | bytes 13762561 | tf_op jit(solution)/shard_map/while/body/eval_jaxpr/add | solution.py:97
  135.9 2.4 fusion.35
  138.3 2.7 fusion.37
  141.0 6.5 %fusion.38 = f32[192,5120]{1,0:T(8,128)S(1)} fusion(s32[5120]{0:T(1024)S(1)} %iota_add_fusion.1, s32[512]{0:T(512)S(1)} %iota_multiply_fusion, s32[]{:T(128)} %bitcast, bf16[384,3584]{1,0:T(8,128)(2,1)S(1)} %fusion.37), kind=kOutput, calls=%fused_computation.132 | convolution fusion | flops 1053818880 | bytes 4151300 | tf_op jit(solution)/shard_map/dot_general | solution.py:54
  147.5 6.9 %fusion.39 = f32[192,5120]{1,0:T(8,128)S(1)} fusion(s32[]{:T(128)} %bitcast.1, s32[5120]{0:T(1024)S(1)} %iota_add_fusion.1, s32[512]{0:T(512)S(1)} %iota_multiply_fusion, bf16[384,3584]{1,0:T(8,128)(2,1)S(1)} %fusion.37), kind=kOutput, calls=%fused_computation.133 | convolution fusion | flops 1053818880 | bytes 4151300 | tf_op jit(solution)/shard_map/dot_general | solution.py:54
  154.5 6.7 %convolution_add_fusion.11 = f32[192,5120]{1,0:T(8,128)S(1)} fusion(f32[192,5120]{1,0:T(8,128)S(1)} %fusion.38, s32[512]{0:T(512)S(1)} %add_multiply_fusion.6, s32[5120]{0:T(1024)S(1)} %iota_add_fusion.1, s32[]{:T(128)} %bitcast, bf16[384,3584]{1,0:T(8,128)(2,1)S(1)} %fusion.37), kind=kOutput, calls=%fused_computation.128 | convolution fusion | flops 1054801920 | bytes 8083460 | tf_op jit(solution)/shard_map/dot_general | solution.py:54
  161.1 6.9 %convolution_add_fusion.5 = f32[192,5120]{1,0:T(8,128)S(1)} fusion(f32[192,5120]{1,0:T(8,128)S(1)} %fusion.39, s32[]{:T(128)} %bitcast.1, s32[512]{0:T(512)S(1)} %add_multiply_fusion.6, s32[5120]{0:T(1024)S(1)} %iota_add_fusion.1, bf16[384,3584]{1,0:T(8,128)(2,1)S(1)} %fusion.37), kind=kOutput, calls=%fused_computation.122 | convolution fusion | flops 1054801920 | bytes 8083460 | tf_op jit(solution)/shard_map/dot_general | solution.py:54
  168.0 6.7 %convolution_add_fusion.10 = f32[192,5120]{1,0:T(8,128)S(1)} fusion(f32[192,5120]{1,0:T(8,128)S(1)} %convolution_add_fusion.11, s32[512]{0:T(512)S(1)} %add_multiply_fusion.5, s32[5120]{0:T(1024)S(1)} %iota_add_fusion.1, s32[]{:T(128)} %bitcast, bf16[384,3584]{1,0:T(8,128)(2,1)S(1)} %fusion.37), kind=kOutput, calls=%fused_computation.127 | convolution fusion | flops 1054801920 | bytes 8083460 | tf_op jit(solution)/shard_map/dot_general | solution.py:54
  174.7 6.9 %convolution_add_fusion.4 = f32[192,5120]{1,0:T(8,128)S(1)} fusion(f32[192,5120]{1,0:T(8,128)S(1)} %convolution_add_fusion.5, s32[]{:T(128)} %bitcast.1, s32[512]{0:T(512)S(1)} %add_multiply_fusion.5, s32[5120]{0:T(1024)S(1)} %iota_add_fusion.1, bf16[384,3584]{1,0:T(8,128)(2,1)S(1)} %fusion.37), kind=kOutput, calls=%fused_computation.121 | convolution fusion | flops 1054801920 | bytes 8083460 | tf_op jit(solution)/shard_map/dot_general | solution.py:54
  181.6 6.7 %convolution_add_fusion.9 = f32[192,5120]{1,0:T(8,128)S(1)} fusion(f32[192,5120]{1,0:T(8,128)S(1)} %convolution_add_fusion.10, s32[512]{0:T(512)S(1)} %add_multiply_fusion.4, s32[5120]{0:T(1024)S(1)} %iota_add_fusion.1, s32[]{:T(128)} %bitcast, bf16[384,3584]{1,0:T(8,128)(2,1)S(1)} %fusion.37), kind=kOutput, calls=%fused_computation.126 | convolution fusion | flops 1054801920 | bytes 8083460 | tf_op jit(solution)/shard_map/dot_general | solution.py:54
  188.3 7.1 %convolution_add_fusion.3 = f32[192,5120]{1,0:T(8,128)S(1)} fusion(f32[192,5120]{1,0:T(8,128)S(1)} %convolution_add_fusion.4, s32[]{:T(128)} %bitcast.1, s32[512]{0:T(512)S(1)} %add_multiply_fusion.4, s32[5120]{0:T(1024)S(1)} %iota_add_fusion.1, bf16[384,3584]{1,0:T(8,128)(2,1)S(1)} %fusion.37), kind=kOutput, calls=%fused_computation.120 | convolution fusion | flops 1054801920 | bytes 8083460 | tf_op jit(solution)/shard_map/dot_general | solution.py:54
  195.4 6.7 %convolution_add_fusion.8 = f32[192,5120]{1,0:T(8,128)S(1)} fusion(f32[192,5120]{1,0:T(8,128)S(1)} %convolution_add_fusion.9, s32[512]{0:T(512)S(1)} %add_multiply_fusion.3, s32[5120]{0:T(1024)S(1)} %iota_add_fusion.1, s32[]{:T(128)} %bitcast, bf16[384,3584]{1,0:T(8,128)(2,1)S(1)} %fusion.37), kind=kOutput, calls=%fused_computation.125 | convolution fusion | flops 1054801920 | bytes 8083460 | tf_op jit(solution)/shard_map/dot_general | solution.py:54
  202.1 6.9 %convolution_add_fusion.2 = f32[192,5120]{1,0:T(8,128)S(1)} fusion(f32[192,5120]{1,0:T(8,128)S(1)} %convolution_add_fusion.3, s32[]{:T(128)} %bitcast.1, s32[512]{0:T(512)S(1)} %add_multiply_fusion.3, s32[5120]{0:T(1024)S(1)} %iota_add_fusion.1, bf16[384,3584]{1,0:T(8,128)(2,1)S(1)} %fusion.37), kind=kOutput, calls=%fused_computation.119 | convolution fusion | flops 1054801920 | bytes 8083460 | tf_op jit(solution)/shard_map/dot_general | solution.py:54
  209.0 6.9 %convolution_add_fusion.7 = f32[192,5120]{1,0:T(8,128)S(1)} fusion(f32[192,5120]{1,0:T(8,128)S(1)} %convolution_add_fusion.8, s32[512]{0:T(512)S(1)} %copy-done.2, s32[5120]{0:T(1024)S(1)} %iota_add_fusion.1, s32[]{:T(128)} %bitcast, bf16[384,3584]{1,0:T(8,128)(2,1)S(1)} %fusion.37), kind=kOutput, calls=%fused_computation.124 | convolution fusion | flops 1054801920 | bytes 8083460 | tf_op jit(solution)/shard_map/dot_general | solution.py:54
  215.9 6.7 %convolution_add_fusion.1 = f32[192,5120]{1,0:T(8,128)S(1)} fusion(f32[192,5120]{1,0:T(8,128)S(1)} %convolution_add_fusion.2, s32[]{:T(128)} %bitcast.1, s32[512]{0:T(512)S(1)} %copy-done.2, s32[5120]{0:T(1024)S(1)} %iota_add_fusion.1, bf16[384,3584]{1,0:T(8,128)(2,1)S(1)} %fusion.37), kind=kOutput, calls=%fused_computation.118 | convolution fusion | flops 1054801920 | bytes 8083460 | tf_op jit(solution)/shard_map/dot_general | solution.py:54
  222.6 8.8 %convolution_add_fusion.6 = f32[192,5120]{1,0:T(8,128)} fusion(f32[192,5120]{1,0:T(8,128)S(1)} %convolution_add_fusion.7, s32[512]{0:T(512)S(1)} %copy-done.1, s32[5120]{0:T(1024)S(1)} %iota_add_fusion.1, s32[]{:T(128)} %bitcast, bf16[384,3584]{1,0:T(8,128)(2,1)S(1)} %fusion.37), kind=kOutput, calls=%fused_computation.123 | convolution fusion | flops 1054801920 | bytes 8083460 | tf_op jit(solution)/shard_map/dot_general | solution.py:54
  231.5 8.6 %convolution_add_fusion = f32[192,5120]{1,0:T(8,128)} fusion(f32[192,5120]{1,0:T(8,128)S(1)} %convolution_add_fusion.1, s32[]{:T(128)} %bitcast.1, s32[512]{0:T(512)S(1)} %copy-done.1, s32[5120]{0:T(1024)S(1)} %iota_add_fusion.1, bf16[384,3584]{1,0:T(8,128)(2,1)S(1)} %fusion.37), kind=kOutput, calls=%fused_computation.117 | convolution fusion | flops 1054801920 | bytes 8083460 | tf_op jit(solution)/shard_map/dot_general | solution.py:54
  240.0 22.8 %multiply_convert_fusion.14 = bf16[384,5120]{1,0:T(8,128)(2,1)} fusion(f32[192,5120]{1,0:T(8,128)} %convolution_add_fusion, f32[192,5120]{1,0:T(8,128)} %convolution_add_fusion.6, bf16[384,3584]{1,0:T(8,128)(2,1)S(1)} %fusion.37, bf16[3584,5120]{1,0:T(8,128)(2,1)} %all-gather.5.cloned.1.call-done, f32[384]{0:T(512)S(1)} %copy-done), kind=kOutput, calls=%fused_computation.114 | convolution fusion | flops 14108590080 | bytes 51250688 | tf_op jit(solution)/shard_map/dot_general | solution.py:45
  (47 shorter events, 9.3 us)
Async XLA Ops:
  7.2 128.7 %all-gather.3.cloned.1.call-start = ((), (), s32[]{:S(2)}) async-start(), calls=%async_computation | async-start | bytes 4128768 | tf_op jit(solution)/shard_map/all_gather | solution.py:75
  7.9 232.1 %all-gather.5.cloned.1.call-start = ((), (), s32[]{:S(2)}) async-start(), calls=%async_computation.1 | async-start | bytes 38993920 | tf_op jit(solution)/shard_map/all_gather | solution.py:83
  202.1 6.9 %copy-start.2 = (s32[512]{0:T(512)S(1)}, s32[512]{0:T(512)}, u32[]{:S(2)}) copy-start(s32[512]{0:T(512)} %add_multiply_fusion.2) | copy-start | bytes 6148
  215.9 6.7 %copy-start.1 = (s32[512]{0:T(512)S(1)}, s32[512]{0:T(512)}, u32[]{:S(2)}) copy-start(s32[512]{0:T(512)} %add_multiply_fusion.1) | copy-start | bytes 6148
  231.4 8.6 %copy-start = (f32[384]{0:T(512)S(1)}, f32[384]{0:T(512)}, u32[]{:S(2)}) copy-start(f32[384]{0:T(512)} %mul.291) | copy-start | bytes 4612
Sparse Core Ops, SparseCore 0:
  9.5 43.1 all-gather.2
  54.4 182.8 all-gather.4
where the time goes:
time: 274 us; the launch traced here: 270 us
  matrix products  122 us (45%)
  other arithmetic  110 us (40%)
  between operations  17.2 us (6%)
  blocking collectives  13.7 us (5%)
  local copies, waits for them, and re-layouts  6.17 us (2%)
    dot_general x14, matrix products, make_fold(): jnp.dot(pair_rows[:, lower_row:lower_row + height], sample, preferred_ele...  98.9 us
    reduce_sum x2, other arithmetic, accumulate(): jnp.sum(group_coefs[:, None, None] * samples, axis=0)  89.4 us
    dot_general x1, matrix products, make_fold(): base_sum = jnp.dot(normed, segment, preferred_element_type=jnp.float32)  22.8 us
    unnamed x1, blocking collectives  13.7 us
    add x2, other arithmetic, accumulate(): running + jnp.sum(group_coefs[:, None, None] * samples, axis=0)  12.1 us
  transfers between devices with their start and end apart: 2, of which 0 were waited for; matrix products, arithmetic and copies ran while one was open for 79% of the time, Pallas kernels for 0%

commit v1 on v0

v1 whole, which is shorter than its diff:
```python
import functools

import jax
import jax.numpy as jnp
from jax import lax
from jax.experimental import pallas as pl
from jax.experimental.pallas import tpu as pltpu
from jax.sharding import PartitionSpec as P

FFW = 10240
ROWS = 96
CHUNKS = 2

noise_scale = 0.01
mix_seed = -1640531535
mix_first = -2048144789
mix_second = -1028477387


def byte_sum(hashed):
    hashed = hashed ^ lax.shift_right_logical(hashed, 16)
    hashed = hashed * jnp.int32(mix_first)
    hashed = hashed ^ lax.shift_right_logical(hashed, 13)
    hashed = hashed * jnp.int32(mix_second)
    hashed = hashed ^ lax.shift_right_logical(hashed, 16)
    low = hashed.astype(jnp.int16)
    return (low & jnp.int16(255)) + lax.shift_right_logical(low, jnp.int16(8))


def counters(height, width):
    rows = lax.broadcasted_iota(jnp.int32, (height, width), 0)
    return rows * FFW + lax.broadcasted_iota(jnp.int32, (height, width), 1)


def pick(extent, options):
    for option in options:
        if extent % option == 0:
            return option
    return extent


def cost(microseconds):
    return pl.CostEstimate(
        flops=int(microseconds * 1.0e9), bytes_accessed=1 << 20, transcendentals=0
    )


def normalize(tokens, norm_gain):
    values = tokens.astype(jnp.float32)
    factor = lax.rsqrt(jnp.mean(values * values, axis=1, keepdims=True) + 1e-06)
    return (values * factor * norm_gain.astype(jnp.float32)).astype(jnp.bfloat16)


def term_kernel(tile, start_ref, rows_ref, out_ref, first, second):
    slots = (first, second)
    height, width = tile
    steps = rows_ref.shape[1] // height
    origin = start_ref[0] + pl.program_id(0) * width
    grid_ids = counters(height, width)

    def fill(step, slot):
        total = byte_sum(grid_ids + (origin + step * height * FFW))
        slot[...] = (total - jnp.int16(255)).astype(jnp.bfloat16)

    fill(0, slots[0])
    for step in range(steps):
        product = jnp.dot(
            rows_ref[:, step * height : (step + 1) * height],
            slots[step % 2][...],
            preferred_element_type=jnp.float32,
        )
        if step + 1 < steps:
            fill(step + 1, slots[(step + 1) % 2])
        if step == 0:
            out_ref[...] = product
        else:
            out_ref[...] += product


def noise_term(start, rows, width):
    tile = (256, pick(width, (512, 256, 128)))
    count, depth = rows.shape
    return pl.pallas_call(
        functools.partial(term_kernel, tile),
        out_shape=jax.ShapeDtypeStruct((count, width), jnp.float32),
        grid=(width // tile[1],),
        in_specs=[
            pl.BlockSpec(memory_space=pltpu.SMEM),
            pl.BlockSpec((count, depth), lambda j: (0, 0)),
        ],
        out_specs=pl.BlockSpec((count, tile[1]), lambda j: (0, j)),
        scratch_shapes=[pltpu.VMEM(tile, jnp.bfloat16)] * 2,
        compiler_params=pltpu.CompilerParams(vmem_limit_bytes=32 << 20),
        cost_estimate=cost(42),
        name="noise_term",
    )(start, rows)


def estimate_kernel(tile, denominator, starts_ref, ranks_ref, out_ref):
    height, width = tile
    pairs = starts_ref.shape[0]
    column = pl.program_id(0) * out_ref.shape[1]
    across = out_ref.shape[1] // width
    grid_ids = counters(height, width)
    rank_total = lax.fori_loop(0, pairs, lambda p, t: t + ranks_ref[p], jnp.int32(0))

    def one(index, carry):
        row = pl.multiple_of(index // across * height, height)
        lane = pl.multiple_of(index % across * width, width)
        ids = grid_ids + (column + row * FFW + lane)

        def add(pair, total):
            part = byte_sum(ids + starts_ref[pair]).astype(jnp.int32)
            return total + ranks_ref[pair] * part

        total = lax.fori_loop(0, pairs, add, jnp.zeros(tile, jnp.int32), unroll=32)
        centred = (total - 255 * rank_total).astype(jnp.float32)
        out_ref[pl.ds(row, height), pl.ds(lane, width)] = centred * (1.0 / denominator)
        return carry

    lax.fori_loop(0, out_ref.shape[0] // height * across, one, 0)


def make_estimate(starts, ranks, rows, width, members):
    block = pick(width, (512, 256, 128))
    tile = (pick(rows, (32, 8)), pick(block, (256, 128)))
    return pl.pallas_call(
        functools.partial(estimate_kernel, tile, 128 * (members - 1) * members * noise_scale),
        out_shape=jax.ShapeDtypeStruct((rows, width), jnp.float32),
        grid=(width // block,),
        in_specs=[pl.BlockSpec(memory_space=pltpu.SMEM)] * 2,
        out_specs=pl.BlockSpec((rows, block), lambda j: (0, j)),
        compiler_params=pltpu.CompilerParams(vmem_limit_bytes=32 << 20),
        cost_estimate=cost(75),
        name="estimate",
    )(starts, ranks)


def project_kernel(spans, offsets_ref, rows_ref, weight_ref, *refs):
    terms, out_ref = refs[:spans], refs[-1]
    base = jnp.dot(rows_ref[...], weight_ref[...], preferred_element_type=jnp.float32)
    span = terms[0].shape[0]
    for index in range(spans):
        for half in range(span // ROWS):
            low = half * ROWS
            scale = (noise_scale / 128) * (1 - 2 * (half % 2))
            value = base[index * span + low : index * span + low + ROWS]
            value = value + scale * terms[index][low : low + ROWS, :]
            value = value / (1.0 + jnp.exp(-value))
            place = pl.multiple_of(offsets_ref[index] + low, 16)
            out_ref[pl.ds(place, ROWS), :] = value.astype(jnp.bfloat16)


def project(offsets, rows, weight, terms, previous, chunk, width):
    count, depth = rows.shape
    part = weight.shape[1]
    block = pick(part, (512, 256, 128))
    first = chunk * (part // block)
    span = terms[0].shape[0]
    operands = [offsets, rows, weight, *terms]
    in_specs = [
        pl.BlockSpec(memory_space=pltpu.SMEM),
        pl.BlockSpec((count, depth), lambda j: (0, 0)),
        pl.BlockSpec((depth, block), lambda j: (0, j)),
    ] + [pl.BlockSpec((span, block), lambda j: (0, j + first))] * len(terms)
    aliases = {}
    if previous is not None:
        aliases = {len(operands): 0}
        operands.append(previous)
        in_specs.append(pl.BlockSpec(memory_space=pl.ANY))
    return pl.pallas_call(
        functools.partial(project_kernel, len(terms)),
        out_shape=jax.ShapeDtypeStruct((count, width), jnp.bfloat16),
        grid=(part // block,),
        in_specs=in_specs,
        out_specs=pl.BlockSpec((count, block), lambda j: (0, j + first)),
        input_output_aliases=aliases,
        compiler_params=pltpu.CompilerParams(vmem_limit_bytes=48 << 20),
        cost_estimate=cost(16 / CHUNKS),
        name="project",
    )(*operands)


def collect(values, axis, size):
    if size & (size - 1):
        return lax.all_gather(values, axis, axis=0, tiled=False)
    place = lax.axis_index(axis)
    block = values[None]
    step = 1
    while step < size:
        other = lax.ppermute(block, axis, [(i, i ^ step) for i in range(size)])
        upper = (place & step) != 0
        block = jnp.concatenate(
            [jnp.where(upper, other, block), jnp.where(upper, block, other)], 0
        )
        step *= 2
    return block


def shards(pops, tps, tokens, norm_gain, weight, pair_seeds, member_ranks):
    owned_rows, width = weight.shape
    pop_index, tp_index = lax.axis_index("pop"), lax.axis_index("tp")
    part = width // CHUNKS
    gathered = [
        lax.all_gather(weight[:, c * part : (c + 1) * part], "pop", axis=0, tiled=True)
        for c in range(CHUNKS)
    ]
    pairs = pair_seeds.shape[0]
    col_start = tp_index * width
    starts = pair_seeds * jnp.int32(mix_seed) + col_start

    span = 2 * ROWS
    if tps == pairs and tokens.shape[0] == span:
        order = [(tp_index + step) % tps for step in range(tps)]
        pieces = [tokens]
        for step in range(1, tps):
            shift = [((i + step) % tps, i) for i in range(tps)]
            pieces.append(lax.ppermute(tokens, "tp", shift))
        pieces = [normalize(piece, norm_gain) for piece in pieces]
    else:
        order = [jnp.int32(step) for step in range(pairs)]
        normed = normalize(lax.all_gather(tokens, "tp", axis=0, tiled=True), norm_gain)
        pieces = [normed[i * span : (i + 1) * span] for i in range(pairs)]
    terms = [
        noise_term(lax.dynamic_slice(starts, (place,), (1,)), piece, width)
        for place, piece in zip(order, pieces)
    ]

    everyone = collect(jnp.concatenate([pair_seeds, member_ranks]), "pop", pops)
    all_seeds = everyone[:, :pairs].reshape(-1)
    all_ranks = everyone[:, pairs:].reshape(-1)
    estimate = make_estimate(
        all_seeds * jnp.int32(mix_seed) + pop_index * (owned_rows * FFW) + col_start,
        all_ranks[0::2] - all_ranks[1::2],
        owned_rows,
        width,
        all_ranks.shape[0],
    )

    offsets = jnp.stack([place * span for place in order]).astype(jnp.int32)
    normed = jnp.concatenate(pieces, 0)
    activated = None
    for chunk in range(CHUNKS):
        activated = project(offsets, normed, gathered[chunk], terms, activated, chunk, width)
    return (activated, estimate)


def solution(mesh):
    placed = (P(("pop", "tp"), None), P(), P("pop", "tp"), P("pop"), P("pop"))
    return jax.shard_map(
        functools.partial(shards, mesh.shape["pop"], mesh.shape["tp"]),
        mesh=mesh,
        in_specs=placed,
        out_specs=(P("pop", "tp"), P("pop", "tp")),
        check_vma=False,
    )
```

time: 274 us -> 228 us (0.83); the launches traced: 270 us -> 228 us
  Pallas kernels: 0 us -> 181 us
  matrix products: 122 us -> 0 us
  other arithmetic: 110 us -> 4.88 us
  blocking collectives: 13.7 us -> 0 us
  waiting for transfers between devices: 1.4 us -> 10.9 us
  starting transfers between devices: 0.08 us -> 8.96 us
  between operations: 17.2 us -> 14.2 us
    pallas_call x0 -> x5, Pallas kernels: none -> 181 us  [the longest x2 77.7 us: noise_term(): pl.pallas_call(functools.partial(term_kernel, tile), out_shape=jax.ShapeD...]
    dot_general x15 -> x0, matrix products: 122 us -> none  [the longest x14 98.9 us: make_fold(): jnp.dot(pair_rows[:, lower_row:lower_row + height], sample, preferred_ele...]
    reduce_sum x2 -> x0, other arithmetic: 89.4 us -> none  [accumulate(): jnp.sum(group_coefs[:, None, None] * samples, axis=0)]
    unnamed x1 -> x0, blocking collectives: 13.7 us -> none
    add x7 -> x2, other arithmetic: 13.1 us -> 0.01 us  [the longest x1 0.01 us: shards(): all_seeds * jnp.int32(mix_seed) + pop_index * (owned_rows * FFW) + col_start]
    ppermute x0 -> x5, starting transfers between devices: none -> 8.88 us  [the longest x4 5.85 us: collect(): other = lax.ppermute(block, axis, [(i, i ^ step) for i in range(size)])]
    ppermute x0 -> x5, waiting for transfers between devices: none -> 6.05 us  [the longest x4 6.05 us: collect(): other = lax.ppermute(block, axis, [(i, i ^ step) for i in range(size)])]
    all_gather x2, waiting for transfers between devices: 0.02 us -> 4.11 us  [shards(): lax.all_gather(weight[:, c * part:(c + 1) * part], 'pop', axis=0, tiled=T...]
  transfers between devices with their start and end apart: 2 -> 7, of which waited for: 0 -> 5; matrix products, arithmetic and copies ran while one was open for 79% -> 3% of each run, Pallas kernels for 0% -> 74%
where the time goes in v1:
time: 228 us
  Pallas kernels  181 us (79%)
  between operations  14.2 us (6%)
  waiting for transfers between devices  10.9 us (5%)
  starting transfers between devices  8.96 us (4%)
  local copies, waits for them, and re-layouts  8.14 us (4%)
  other arithmetic  4.88 us (2%)
    pallas_call x2, Pallas kernels, noise_term(): pl.pallas_call(functools.partial(term_kernel, tile), out_shape=jax.ShapeD...  77.7 us
    pallas_call x1, Pallas kernels, make_estimate(): pl.pallas_call(functools.partial(estimate_kernel, tile, 128 * (members -...  77 us
    pallas_call x2, Pallas kernels, project(): pl.pallas_call(functools.partial(project_kernel, len(terms)), out_shape=j...  26.1 us
    ppermute x4, waiting for transfers between devices, collect(): other = lax.ppermute(block, axis, [(i, i ^ step) for i in range(size)])  6.05 us
    ppermute x4, starting transfers between devices, collect(): other = lax.ppermute(block, axis, [(i, i ^ step) for i in range(size)])  5.85 us
  transfers between devices with their start and end apart: 7, of which 5 were waited for; matrix products, arithmetic and copies ran while one was open for 3% of the time, Pallas kernels for 74%

profile of v1, /device:TPU:0, one launch (start us, length us, event | category | flops | bytes accessed | tf_op | source)
XLA Modules:
  0.0 227.8 jit_solution(17860577831675998134)
XLA Ops:
  7.3 3.2 %fusion.8 = (bf16[224,2560]{1,0:T(8,128)(2,1)}, bf16[224,2560]{1,0:T(8,128)(2,1)}) fusion(bf16[224,5120]{1,0:T(8,128)(2,1)} %param.7), kind=kLoop, calls=%fused_computation.31 | loop fusion | bytes 4587520 | tf_op jit(solution)/shard_map/slice | solution.py:205
  10.6 0.7 all-gather.3.cloned.1.call-update
  11.3 3.0 %collective-permute-start = (bf16[192,3584]{1,0:T(8,128)(2,1)S(1)}, bf16[192,3584]{1,0:T(8,128)(2,1)}, u32[]{:S(2)}, u32[]{:S(2)}) collective-permute-start(bf16[192,3584]{1,0:T(8,128)(2,1)S(1)} %copy-done.2), channel_id=1, source_target_pairs={{1,0},{0,1},{3,2},{2,3},{5,4},{4,5},{7,6},{6,7},{9,8},{8,9},{11,10... | collective-permute-start | bytes 4128776 | tf_op jit(solution)/shard_map/ppermute | solution.py:218
  14.5 0.4 fusion
  14.9 0.6 collective-permute-done.1
  15.6 1.5 collective-permute-start.2
  17.1 2.1 collective-permute-done.2
  19.3 1.6 collective-permute-start.3
  20.9 2.0 collective-permute-done.3
  22.9 2.7 %collective-permute-start.4 = (s32[8,6]{1,0:T(8,128)S(1)}, s32[8,6]{1,0:T(8,128)S(1)}, u32[]{:S(2)}, u32[]{:S(2)}) collective-permute-start(s32[8,6]{1,0:T(8,128)S(1)} %pad_add_fusion.1), channel_id=1, source_target_pairs={{0,16},{2,18},{4,20},{6,22},{8,24},{10,26},{12,28},{14,30},{16,0},... | collective-permute-start | bytes 584 | tf_op jit(solution)/shard_map/ppermute | solution.py:191
  25.6 0.7 fusion.9
  26.2 1.4 collective-permute-done.4
  27.8 0.1 slice.22
  28.2 77.0 %estimate.1 = f32[224,5120]{1,0:T(8,128)} custom-call(s32[32]{0:T(128)S(1)} %add.66.starts_ref, s32[32]{0:T(128)S(1)} %sub.3.ranks_ref), custom_call_target="tpu_custom_call" | custom-call | flops 74999996416 | bytes 1048576 | tf_op jit(solution)/shard_map/estimate/pallas_call | solution.py:127
  105.1 1.7 fusion.3
  106.8 2.3 fusion.2
  109.1 0.2 pad_maximum_fusion.rows_ref
  109.3 38.8 %noise_term.2.refs_0_ = f32[192,5120]{1,0:T(8,128)S(1)} custom-call(s32[1]{0:T(128)} %get-tuple-element.15.start_ref, bf16[192,3584]{1,0:T(8,128)(2,1)S(1)} %get-tuple-element.4.rows_ref), custom_call_target="tpu_custom_call" | custom-call | flops 41999998976 | bytes 1048576 | tf_op jit(solution)/shard_map/noise_term/pallas_call | solution.py:83
  148.1 1.9 copy-done
  150.0 38.9 %noise_term.3.refs_1_ = f32[192,5120]{1,0:T(8,128)S(1)} custom-call(s32[1]{0:T(128)} %get-tuple-element.14.start_ref, bf16[192,3584]{1,0:T(8,128)(2,1)S(1)} %get-tuple-element.5.rows_ref), custom_call_target="tpu_custom_call" | custom-call | flops 41999998976 | bytes 1048576 | tf_op jit(solution)/shard_map/noise_term/pallas_call | solution.py:83
  188.9 1.9 copy-done.1
  190.8 13.1 %project.2.refs_2_ = bf16[384,5120]{1,0:T(8,128)(2,1)} custom-call(s32[2]{0:T(128)S(1)} %pad_add_fusion.4.offsets_ref, bf16[384,3584]{1,0:T(8,128)(2,1)S(1)} %pad_maximum_fusion.rows_ref, bf16[3584,2560]{1,0:T(8,128)(2,1)} %all-gather.5.cloned.1.call-done.weight_ref, f32[192,5120]{1,0:T(8,128)} %copy-done, f32[192,5120]{1,0:T(8,128)} %copy-done.1), custom_call_target="tpu_custom_call" | custom-call | flops 8000000000 | bytes 1048576 | tf_op jit(solution)/shard_map/project/pallas_call | solution.py:171
  203.9 4.1 %all-gather.3.cloned.1.call-done.weight_ref = bf16[3584,2560]{1,0:T(8,128)(2,1)} async-done(((bf16[224,2560]{1,0:T(8,128)(2,1)}), bf16[3584,2560]{1,0:T(8,128)(2,1)}) %all-gather.3.cloned.1.call-update) | async-done | bytes 18350096 | tf_op jit(solution)/shard_map/all_gather | solution.py:205
  208.1 12.9 %project.3 = bf16[384,5120]{1,0:T(8,128)(2,1)} custom-call(s32[2]{0:T(128)S(1)} %pad_add_fusion.4.offsets_ref, bf16[384,3584]{1,0:T(8,128)(2,1)S(1)} %pad_maximum_fusion.rows_ref, bf16[3584,2560]{1,0:T(8,128)(2,1)} %all-gather.3.cloned.1.call-done.weight_ref, f32[192,5120]{1,0:T(8,128)} %copy-done, ...), custom_call_target="tpu_custom_call", output_to_operand_aliasing={{}: (5, {})} | custom-call | flops 8000000000 | bytes 1048576 | tf_op jit(solution)/shard_map/project/pallas_call | solution.py:171
  (35 shorter events, 0.8 us)
Async XLA Ops:
  7.2 4.1 %copy-start.2 = (bf16[192,3584]{1,0:T(8,128)(2,1)S(1)}, bf16[192,3584]{1,0:T(8,128)(2,1)}, u32[]{:S(2)}) copy-start(bf16[192,3584]{1,0:T(8,128)(2,1)} %param.5) | copy-start | bytes 4128772
  7.2 7.1 %copy-start.4 = (s32[2]{0:T(128)S(1)}, s32[2]{0:T(128)}, u32[]{:S(2)}) copy-start(s32[2]{0:T(128)} %param.8) | copy-start | bytes 28
  7.2 7.1 %copy-start.5 = (s32[4]{0:T(128)S(1)}, s32[4]{0:T(128)}, u32[]{:S(2)}) copy-start(s32[4]{0:T(128)} %param.9) | copy-start | bytes 52
  7.2 7.2 %copy-start.3 = (bf16[3584]{0:T(1024)(128)(2,1)S(1)}, bf16[3584]{0:T(1024)(128)(2,1)}, u32[]{:S(2)}) copy-start(bf16[3584]{0:T(1024)(128)(2,1)} %param.6) | copy-start | bytes 21508
  7.2 183.6 %all-gather.5.cloned.1.call-start = ((), (), s32[]{:S(2)}) async-start(), calls=%async_computation.1 | async-start | bytes 19496960 | tf_op jit(solution)/shard_map/all_gather | solution.py:205
  10.5 197.5 %all-gather.3.cloned.1.call-start = ((), (), s32[]{:S(2)}) async-start(), calls=%async_computation | async-start | bytes 19496960 | tf_op jit(solution)/shard_map/all_gather | solution.py:205
  11.3 93.8 %collective-permute-start = (bf16[192,3584]{1,0:T(8,128)(2,1)S(1)}, bf16[192,3584]{1,0:T(8,128)(2,1)}, u32[]{:S(2)}, u32[]{:S(2)}) collective-permute-start(bf16[192,3584]{1,0:T(8,128)(2,1)S(1)} %copy-done.2), channel_id=1, source_target_pairs={{1,0},{0,1},{3,2},{2,3},{5,4},{4,5},{7,6},{6,7},{9,8},{8,9},{11,10... | collective-permute-start | bytes 4128776 | tf_op jit(solution)/shard_map/ppermute | solution.py:218
  14.4 1.1 collective-permute-start.1
  15.6 3.6 %collective-permute-start.2 = (s32[2,6]{1,0:T(2,128)S(1)}, s32[2,6]{1,0:T(2,128)S(1)}, u32[]{:S(2)}, u32[]{:S(2)}) collective-permute-start(s32[2,6]{1,0:T(2,128)S(1)} %pad_add_fusion.3), channel_id=1, source_target_pairs={{0,4},{2,6},{4,0},{6,2},{8,12},{10,14},{12,8},{14,10},{16,20},{18,... | collective-permute-start | bytes 152 | tf_op jit(solution)/shard_map/ppermute | solution.py:191
  19.3 3.7 %collective-permute-start.3 = (s32[4,6]{1,0:T(4,128)S(1)}, s32[4,6]{1,0:T(4,128)S(1)}, u32[]{:S(2)}, u32[]{:S(2)}) collective-permute-start(s32[4,6]{1,0:T(4,128)S(1)} %pad_add_fusion.2), channel_id=1, source_target_pairs={{0,8},{2,10},{4,12},{6,14},{8,0},{10,2},{12,4},{14,6},{16,24},{18,... | collective-permute-start | bytes 296 | tf_op jit(solution)/shard_map/ppermute | solution.py:191
  22.9 4.7 %collective-permute-start.4 = (s32[8,6]{1,0:T(8,128)S(1)}, s32[8,6]{1,0:T(8,128)S(1)}, u32[]{:S(2)}, u32[]{:S(2)}) collective-permute-start(s32[8,6]{1,0:T(8,128)S(1)} %pad_add_fusion.1), channel_id=1, source_target_pairs={{0,16},{2,18},{4,20},{6,22},{8,24},{10,26},{12,28},{14,30},{16,0},... | collective-permute-start | bytes 584 | tf_op jit(solution)/shard_map/ppermute | solution.py:191
  148.1 1.9 copy-start
  188.9 1.9 copy-start.1
Sparse Core Ops, SparseCore 0:
  10.6 99.3 all-gather.4
  111.6 96.4 all-gather.2

commit v2 on v1

--- a/solution.py
+++ b/solution.py
@@ -1,4 +1,5 @@
 import functools
+import math
 
 import jax
 import jax.numpy as jnp
@@ -9,7 +10,6 @@
 
 FFW = 10240
 ROWS = 96
-CHUNKS = 2
 
 noise_scale = 0.01
 mix_seed = -1640531535
@@ -90,7 +90,7 @@
         ],
         out_specs=pl.BlockSpec((count, tile[1]), lambda j: (0, j)),
         scratch_shapes=[pltpu.VMEM(tile, jnp.bfloat16)] * 2,
-        compiler_params=pltpu.CompilerParams(vmem_limit_bytes=32 << 20),
+        compiler_params=pltpu.CompilerParams(vmem_limit_bytes=56 << 20),
         cost_estimate=cost(42),
         name="noise_term",
     )(start, rows)
@@ -130,7 +130,7 @@
         grid=(width // block,),
         in_specs=[pl.BlockSpec(memory_space=pltpu.SMEM)] * 2,
         out_specs=pl.BlockSpec((rows, block), lambda j: (0, j)),
-        compiler_params=pltpu.CompilerParams(vmem_limit_bytes=32 << 20),
+        compiler_params=pltpu.CompilerParams(vmem_limit_bytes=56 << 20),
         cost_estimate=cost(75),
         name="estimate",
     )(starts, ranks)
@@ -151,11 +151,11 @@
             out_ref[pl.ds(place, ROWS), :] = value.astype(jnp.bfloat16)
 
 
-def project(offsets, rows, weight, terms, previous, chunk, width):
+def project(offsets, rows, weight, terms, previous, column, width):
     count, depth = rows.shape
     part = weight.shape[1]
-    block = pick(part, (512, 256, 128))
-    first = chunk * (part // block)
+    block = pick(math.gcd(part, column), (512, 256, 128) if column == 0 else (256, 128))
+    first = column // block
     span = terms[0].shape[0]
     operands = [offsets, rows, weight, *terms]
     in_specs = [
@@ -175,35 +175,47 @@
         in_specs=in_specs,
         out_specs=pl.BlockSpec((count, block), lambda j: (0, j + first)),
         input_output_aliases=aliases,
-        compiler_params=pltpu.CompilerParams(vmem_limit_bytes=48 << 20),
-        cost_estimate=cost(16 / CHUNKS),
+        compiler_params=pltpu.CompilerParams(vmem_limit_bytes=56 << 20),
+        cost_estimate=cost(part / 200),
         name="project",
     )(*operands)
 
 
-def collect(values, axis, size):
+def spread(held, digit):
+    ordered = []
+    for value in range(len(held)):
+        piece = held[0]
+        for k in range(1, len(held)):
+            piece = jnp.where((digit ^ k) == value, held[k], piece)
+        ordered.append(piece)
+    return jnp.concatenate(ordered, 0)
+
+
+def collect(values, axis, size, anchors):
     if size & (size - 1):
-        return lax.all_gather(values, axis, axis=0, tiled=False)
-    place = lax.axis_index(axis)
-    block = values[None]
-    step = 1
+        return lax.all_gather(values, axis, axis=0, tiled=False), anchors
+    block, step, stage, anchors = values[None], 1, 0, list(anchors)
     while step < size:
-        other = lax.ppermute(block, axis, [(i, i ^ step) for i in range(size)])
-        upper = (place & step) != 0
-        block = jnp.concatenate(
-            [jnp.where(upper, other, block), jnp.where(upper, block, other)], 0
-        )
-        step *= 2
-    return block
+        radix = 4 if size // step >= 4 else 2
+        held = [block] + [
+            lax.ppermute(block, axis, [(i, i ^ (k * step)) for i in range(size)])
+            for k in range(1, radix)
+        ]
+        if stage < len(anchors):
+            held, anchors[stage] = lax.optimization_barrier((held, anchors[stage]))
+        block = spread(held, lax.axis_index(axis) // step % radix)
+        step *= radix
+        stage += 1
+    return block, anchors
 
 
 def shards(pops, tps, tokens, norm_gain, weight, pair_seeds, member_ranks):
     owned_rows, width = weight.shape
     pop_index, tp_index = lax.axis_index("pop"), lax.axis_index("tp")
-    part = width // CHUNKS
+    split = width * 4 // 5 // 128 * 128
     gathered = [
-        lax.all_gather(weight[:, c * part : (c + 1) * part], "pop", axis=0, tiled=True)
-        for c in range(CHUNKS)
+        lax.all_gather(weight[:, :split], "pop", axis=0, tiled=True),
+        lax.all_gather(weight[:, split:], "pop", axis=0, tiled=True),
     ]
     pairs = pair_seeds.shape[0]
     col_start = tp_index * width
@@ -212,21 +224,24 @@
     span = 2 * ROWS
     if tps == pairs and tokens.shape[0] == span:
         order = [(tp_index + step) % tps for step in range(tps)]
-        pieces = [tokens]
-        for step in range(1, tps):
-            shift = [((i + step) % tps, i) for i in range(tps)]
-            pieces.append(lax.ppermute(tokens, "tp", shift))
-        pieces = [normalize(piece, norm_gain) for piece in pieces]
+        arrived = [tokens] + [
+            lax.ppermute(tokens, "tp", [((i + step) % tps, i) for i in range(tps)])
+            for step in range(1, tps)
+        ]
     else:
         order = [jnp.int32(step) for step in range(pairs)]
-        normed = normalize(lax.all_gather(tokens, "tp", axis=0, tiled=True), norm_gain)
-        pieces = [normed[i * span : (i + 1) * span] for i in range(pairs)]
-    terms = [
-        noise_term(lax.dynamic_slice(starts, (place,), (1,)), piece, width)
-        for place, piece in zip(order, pieces)
-    ]
-
-    everyone = collect(jnp.concatenate([pair_seeds, member_ranks]), "pop", pops)
+        whole = lax.all_gather(tokens, "tp", axis=0, tiled=True)
+        arrived = [whole[i * span : (i + 1) * span] for i in range(pairs)]
+    pieces, terms = [], []
+    for place, piece in zip(order, arrived):
+        if terms:
+            piece, terms[-1] = lax.optimization_barrier((piece, terms[-1]))
+        pieces.append(normalize(piece, norm_gain))
+        start = lax.dynamic_slice(starts, (place,), (1,))
+        terms.append(noise_term(start, pieces[-1], width))
+
+    everyone, terms = collect(jnp.concatenate([pair_seeds, member_ranks]), "pop", pops, terms)
+    everyone, terms = lax.optimization_barrier((everyone, terms))
     all_seeds = everyone[:, :pairs].reshape(-1)
     all_ranks = everyone[:, pairs:].reshape(-1)
     estimate = make_estimate(
@@ -239,9 +254,11 @@
 
     offsets = jnp.stack([place * span for place in order]).astype(jnp.int32)
     normed = jnp.concatenate(pieces, 0)
-    activated = None
-    for chunk in range(CHUNKS):
-        activated = project(offsets, normed, gathered[chunk], terms, activated, chunk, width)
+    terms, estimate = lax.optimization_barrier((terms, estimate))
+    activated, first = None, 0
+    for piece in gathered:
+        activated = project(offsets, normed, piece, terms, activated, first, width)
+        first += piece.shape[1]
     return (activated, estimate)
 
 

time: 228 us -> 247 us (1.083)
  waiting for transfers between devices: 10.9 us -> 21.8 us
  Pallas kernels: 181 us -> 188 us
    all_gather x2, waiting for transfers between devices: 4.11 us -> 21.7 us  [the longest x1 21.7 us: shards(): lax.all_gather(weight[:, split:], 'pop', axis=0, tiled=True)]
    ppermute x5 -> x7, waiting for transfers between devices: 6.05 us -> 0.02 us  [the longest x6 0.02 us: collect(): lax.ppermute(block, axis, [(i, i ^ k * step) for i in range(size)])]
    pallas_call x2, Pallas kernels: 77.7 us -> 82.3 us  [noise_term(): pl.pallas_call(functools.partial(term_kernel, tile), out_shape=jax.ShapeD...]
    unnamed x12, local copies, waits for them, and re-layouts: 3.82 us -> 0.02 us
    pallas_call x2, Pallas kernels: 26.1 us -> 29 us  [project(): pl.pallas_call(functools.partial(project_kernel, len(terms)), out_shape=j...]
    ppermute x5 -> x7, starting transfers between devices: 8.88 us -> 9.3 us  [the longest x6 7.54 us: collect(): lax.ppermute(block, axis, [(i, i ^ k * step) for i in range(size)])]
  transfers between devices with their start and end apart: 7 -> 9, of which waited for: 5 -> 1; matrix products, arithmetic and copies ran while one was open for 3% -> 4% of each run, Pallas kernels for 74% -> 73%
where the time goes in v2:
time: 247 us
  Pallas kernels  188 us (76%)
  waiting for transfers between devices  21.8 us (9%)
  between operations  14.2 us (6%)
  starting transfers between devices  9.38 us (4%)
  other arithmetic  6.81 us (3%)
  local copies, waits for them, and re-layouts  6.49 us (3%)
    pallas_call x2, Pallas kernels, noise_term(): pl.pallas_call(functools.partial(term_kernel, tile), out_shape=jax.ShapeD...  82.3 us
    pallas_call x1, Pallas kernels, make_estimate(): pl.pallas_call(functools.partial(estimate_kernel, tile, 128 * (members -...  77.1 us
    pallas_call x2, Pallas kernels, project(): pl.pallas_call(functools.partial(project_kernel, len(terms)), out_shape=j...  29 us
    all_gather x1, waiting for transfers between devices, shards(): lax.all_gather(weight[:, split:], 'pop', axis=0, tiled=True)  21.7 us
    ppermute x6, starting transfers between devices, collect(): lax.ppermute(block, axis, [(i, i ^ k * step) for i in range(size)])  7.54 us
  transfers between devices with their start and end apart: 9, of which 1 were waited for; matrix products, arithmetic and copies ran while one was open for 4% of the time, Pallas kernels for 73%

profile of v2, /device:TPU:0, one launch (start us, length us, event | category | flops | bytes accessed | tf_op | source)
XLA Modules:
  0.0 247.0 jit_solution(7753479852575202158)
XLA Ops:
  7.2 3.0 %slice.23 = bf16[224,4096]{1,0:T(8,128)(2,1)} slice(bf16[224,5120]{1,0:T(8,128)(2,1)} %param.7), slice={[0:224], [0:4096]} | slice | bytes 3670016 | tf_op jit(solution)/shard_map/slice | solution.py:217
  10.4 0.5 collective-permute-start.1
  10.9 2.6 %collective-permute-start.2 = (s32[1,6]{1,0:T(1,128)S(1)}, s32[1,6]{1,0:T(1,128)S(1)}, u32[]{:S(2)}, u32[]{:S(2)}) collective-permute-start(s32[1,6]{1,0:T(1,128)S(1)} %add_bitcast_fusion), channel_id=1, source_target_pairs={{0,4},{2,6},{4,0},{6,2},{8,12},{10,14},{12,8},{14,10},{16,20},{18,... | collective-permute-start | bytes 80 | tf_op jit(solution)/shard_map/ppermute | solution.py:201
  13.5 1.8 collective-permute-start
  15.3 1.8 slice.18
  17.2 0.4 fusion
  17.6 1.5 fusion.2.rows_ref
  19.0 0.6 fusion.6
  19.6 41.1 %noise_term.2.refs_0_ = f32[192,5120]{1,0:T(8,128)} custom-call(s32[1]{0:T(128)} %get-tuple-element.47.start_ref, bf16[192,3584]{1,0:T(8,128)(2,1)} %fusion.2.rows_ref), custom_call_target="tpu_custom_call" | custom-call | flops 41999998976 | bytes 1048576 | tf_op jit(solution)/shard_map/noise_term/pallas_call | solution.py:83
  60.7 0.6 pad_add_fusion.2.offsets_ref
  61.4 1.7 collective-permute-start.4
  63.0 2.6 %collective-permute-start.5 = (s32[4,6]{1,0:T(4,128)S(1)}, s32[4,6]{1,0:T(4,128)S(1)}, u32[]{:S(2)}, u32[]{:S(2)}) collective-permute-start(s32[4,6]{1,0:T(4,128)S(1)} %pad_add_fusion.1), channel_id=1, source_target_pairs={{0,16},{2,18},{4,20},{6,22},{8,24},{10,26},{12,28},{14,30},{16,0},... | collective-permute-start | bytes 296 | tf_op jit(solution)/shard_map/ppermute | solution.py:201
  65.6 0.2 collective-permute-start.6
  65.8 0.4 fusion.3
  66.2 1.5 fusion.5.rows_ref
  67.7 41.2 %noise_term.3.refs_1_ = f32[192,5120]{1,0:T(8,128)} custom-call(s32[1]{0:T(128)} %get-tuple-element.46.start_ref, bf16[192,3584]{1,0:T(8,128)(2,1)} %fusion.5.rows_ref), custom_call_target="tpu_custom_call" | custom-call | flops 41999998976 | bytes 1048576 | tf_op jit(solution)/shard_map/noise_term/pallas_call | solution.py:83
  108.9 1.8 pad_maximum_fusion.rows_ref
  110.9 0.1 slice.21
  111.2 0.6 add.76.starts_ref
  111.8 0.6 sub.9.ranks_ref
  112.4 77.1 %estimate.1 = f32[224,5120]{1,0:T(8,128)} custom-call(s32[32]{0:T(128)} %add.76.starts_ref, s32[32]{0:T(128)} %sub.9.ranks_ref), custom_call_target="tpu_custom_call" | custom-call | flops 74999996416 | bytes 1048576 | tf_op jit(solution)/shard_map/estimate/pallas_call | solution.py:127
  189.4 21.0 %project.2.refs_2_ = bf16[384,5120]{1,0:T(8,128)(2,1)} custom-call(s32[2]{0:T(128)} %pad_add_fusion.2.offsets_ref, bf16[384,3584]{1,0:T(8,128)(2,1)} %pad_maximum_fusion.rows_ref, bf16[3584,4096]{1,0:T(8,128)(2,1)} %all-gather.5.cloned.1.call-done.weight_ref, f32[192,5120]{1,0:T(8,128)} %noise_term.2.refs_0_, f32[192,5120]{1,0:T(8,128)} %noise_term.3.refs_1_), custom_call_target="tpu_custom_call" | custom-call | flops 20480000000 | bytes 1048576 | tf_op jit(solution)/shard_map/project/pallas_call | solution.py:171
  210.5 21.7 %all-gather.3.cloned.1.call-done.weight_ref = bf16[3584,1024]{1,0:T(8,128)(2,1)} async-done(((bf16[224,1024]{1,0:T(8,128)(2,1)}), bf16[3584,1024]{1,0:T(8,128)(2,1)}) %all-gather.3.cloned.1.call-update) | async-done | bytes 7340048 | tf_op jit(solution)/shard_map/all_gather | solution.py:218
  232.2 8.0 %project.3 = bf16[384,5120]{1,0:T(8,128)(2,1)} custom-call(s32[2]{0:T(128)} %pad_add_fusion.2.offsets_ref, bf16[384,3584]{1,0:T(8,128)(2,1)} %pad_maximum_fusion.rows_ref, bf16[3584,1024]{1,0:T(8,128)(2,1)} %all-gather.3.cloned.1.call-done.weight_ref, f32[192,5120]{1,0:T(8,128)} %noise_term.2.refs_0_, ...), custom_call_target="tpu_custom_call", output_to_operand_aliasing={{}: (5, {})} | custom-call | flops 5120000000 | bytes 1048576 | tf_op jit(solution)/shard_map/project/pallas_call | solution.py:171
  (38 shorter events, 0.7 us)
Async XLA Ops:
  7.2 3.2 %copy-start.5 = (s32[2]{0:T(128)S(1)}, s32[2]{0:T(128)}, u32[]{:S(2)}) copy-start(s32[2]{0:T(128)} %param.8) | copy-start | bytes 28
  7.2 3.2 %copy-start.4 = (s32[4]{0:T(128)S(1)}, s32[4]{0:T(128)}, u32[]{:S(2)}) copy-start(s32[4]{0:T(128)} %param.9) | copy-start | bytes 52
  7.2 6.3 %copy-start = (bf16[192,3584]{1,0:T(8,128)(2,1)S(1)}, bf16[192,3584]{1,0:T(8,128)(2,1)}, u32[]{:S(2)}) copy-start(bf16[192,3584]{1,0:T(8,128)(2,1)} %param.5) | copy-start | bytes 4128772
  7.2 182.2 %all-gather.5.cloned.1.call-start = ((), (), s32[]{:S(2)}) async-start(), calls=%async_computation.1 | async-start | bytes 31195136 | tf_op jit(solution)/shard_map/all_gather | solution.py:217
  10.3 7.3 %copy-start.3 = (bf16[3584]{0:T(1024)(128)(2,1)S(1)}, bf16[3584]{0:T(1024)(128)(2,1)}, u32[]{:S(2)}) copy-start(bf16[3584]{0:T(1024)(128)(2,1)} %param.6) | copy-start | bytes 21508
  10.3 221.9 %all-gather.3.cloned.1.call-start = ((), (), s32[]{:S(2)}) async-start(), calls=%async_computation | async-start | bytes 7798784 | tf_op jit(solution)/shard_map/all_gather | solution.py:218
  10.4 50.9 %collective-permute-start.1 = (s32[1,6]{1,0:T(1,128)S(1)}, s32[1,6]{1,0:T(1,128)S(1)}, u32[]{:S(2)}, u32[]{:S(2)}) collective-permute-start(s32[1,6]{1,0:T(1,128)S(1)} %add_bitcast_fusion), channel_id=1, source_target_pairs={{0,2},{2,0},{4,6},{6,4},{8,10},{10,8},{12,14},{14,12},{16,18},{18,... | collective-permute-start | bytes 80 | tf_op jit(solution)/shard_map/ppermute | solution.py:201
  10.9 50.4 %collective-permute-start.2 = (s32[1,6]{1,0:T(1,128)S(1)}, s32[1,6]{1,0:T(1,128)S(1)}, u32[]{:S(2)}, u32[]{:S(2)}) collective-permute-start(s32[1,6]{1,0:T(1,128)S(1)} %add_bitcast_fusion), channel_id=1, source_target_pairs={{0,4},{2,6},{4,0},{6,2},{8,12},{10,14},{12,8},{14,10},{16,20},{18,... | collective-permute-start | bytes 80 | tf_op jit(solution)/shard_map/ppermute | solution.py:201
  13.5 47.9 %collective-permute-start.3 = (s32[1,6]{1,0:T(1,128)S(1)}, s32[1,6]{1,0:T(1,128)S(1)}, u32[]{:S(2)}, u32[]{:S(2)}) collective-permute-start(s32[1,6]{1,0:T(1,128)S(1)} %add_bitcast_fusion), channel_id=1, source_target_pairs={{0,6},{2,4},{4,2},{6,0},{8,14},{10,12},{12,10},{14,8},{16,22},{18,... | collective-permute-start | bytes 80 | tf_op jit(solution)/shard_map/ppermute | solution.py:201
  13.5 47.8 %collective-permute-start = (bf16[192,3584]{1,0:T(8,128)(2,1)S(1)}, bf16[192,3584]{1,0:T(8,128)(2,1)S(1)}, u32[]{:S(2)}, u32[]{:S(2)}) collective-permute-start(bf16[192,3584]{1,0:T(8,128)(2,1)S(1)} %copy-done), channel_id=1, source_target_pairs={{1,0},{0,1},{3,2},{2,3},{5,4},{4,5},{7,6},{6,7},{9,8},{8,9},{11,10... | collective-permute-start | bytes 4128776 | tf_op jit(solution)/shard_map/ppermute | solution.py:228
  61.4 49.3 %collective-permute-start.4 = (s32[4,6]{1,0:T(4,128)S(1)}, s32[4,6]{1,0:T(4,128)S(1)}, u32[]{:S(2)}, u32[]{:S(2)}) collective-permute-start(s32[4,6]{1,0:T(4,128)S(1)} %pad_add_fusion.1), channel_id=1, source_target_pairs={{0,8},{2,10},{4,12},{6,14},{8,0},{10,2},{12,4},{14,6},{16,24},{18,... | collective-permute-start | bytes 296 | tf_op jit(solution)/shard_map/ppermute | solution.py:201
  63.0 47.7 %collective-permute-start.5 = (s32[4,6]{1,0:T(4,128)S(1)}, s32[4,6]{1,0:T(4,128)S(1)}, u32[]{:S(2)}, u32[]{:S(2)}) collective-permute-start(s32[4,6]{1,0:T(4,128)S(1)} %pad_add_fusion.1), channel_id=1, source_target_pairs={{0,16},{2,18},{4,20},{6,22},{8,24},{10,26},{12,28},{14,30},{16,0},... | collective-permute-start | bytes 296 | tf_op jit(solution)/shard_map/ppermute | solution.py:201
  65.6 45.1 %collective-permute-start.6 = (s32[4,6]{1,0:T(4,128)S(1)}, s32[4,6]{1,0:T(4,128)S(1)}, u32[]{:S(2)}, u32[]{:S(2)}) collective-permute-start(s32[4,6]{1,0:T(4,128)S(1)} %pad_add_fusion.1), channel_id=1, source_target_pairs={{0,24},{2,26},{4,28},{6,30},{8,16},{10,18},{12,20},{14,22},{16,8},... | collective-permute-start | bytes 296 | tf_op jit(solution)/shard_map/ppermute | solution.py:201
  67.7 41.2 %copy-start.1 = (bf16[192,3584]{1,0:T(8,128)(2,1)S(1)}, bf16[192,3584]{1,0:T(8,128)(2,1)}, u32[]{:S(2)}) copy-start(bf16[192,3584]{1,0:T(8,128)(2,1)} %fusion.2.rows_ref) | copy-start | bytes 4128772
  67.7 41.2 %copy-start.2 = (bf16[192,3584]{1,0:T(8,128)(2,1)S(1)}, bf16[192,3584]{1,0:T(8,128)(2,1)}, u32[]{:S(2)}) copy-start(bf16[192,3584]{1,0:T(8,128)(2,1)} %fusion.5.rows_ref) | copy-start | bytes 4128772
Sparse Core Ops, SparseCore 0:
  10.4 151.1 all-gather.4
  163.9 68.2 all-gather.2

commit v3 on v2

--- a/solution.py
+++ b/solution.py
@@ -1,5 +1,4 @@
 import functools
-import math
 
 import jax
 import jax.numpy as jnp
@@ -151,34 +150,26 @@
             out_ref[pl.ds(place, ROWS), :] = value.astype(jnp.bfloat16)
 
 
-def project(offsets, rows, weight, terms, previous, column, width):
+def project(offsets, rows, weight, terms):
     count, depth = rows.shape
-    part = weight.shape[1]
-    block = pick(math.gcd(part, column), (512, 256, 128) if column == 0 else (256, 128))
-    first = column // block
+    width = weight.shape[1]
+    block = pick(width, (1024, 256, 128))
     span = terms[0].shape[0]
-    operands = [offsets, rows, weight, *terms]
-    in_specs = [
-        pl.BlockSpec(memory_space=pltpu.SMEM),
-        pl.BlockSpec((count, depth), lambda j: (0, 0)),
-        pl.BlockSpec((depth, block), lambda j: (0, j)),
-    ] + [pl.BlockSpec((span, block), lambda j: (0, j + first))] * len(terms)
-    aliases = {}
-    if previous is not None:
-        aliases = {len(operands): 0}
-        operands.append(previous)
-        in_specs.append(pl.BlockSpec(memory_space=pl.ANY))
     return pl.pallas_call(
         functools.partial(project_kernel, len(terms)),
         out_shape=jax.ShapeDtypeStruct((count, width), jnp.bfloat16),
-        grid=(part // block,),
-        in_specs=in_specs,
-        out_specs=pl.BlockSpec((count, block), lambda j: (0, j + first)),
-        input_output_aliases=aliases,
+        grid=(width // block,),
+        in_specs=[
+            pl.BlockSpec(memory_space=pltpu.SMEM),
+            pl.BlockSpec((count, depth), lambda j: (0, 0)),
+            pl.BlockSpec((depth, block), lambda j: (0, j)),
+        ]
+        + [pl.BlockSpec((span, block), lambda j: (0, j))] * len(terms),
+        out_specs=pl.BlockSpec((count, block), lambda j: (0, j)),
         compiler_params=pltpu.CompilerParams(vmem_limit_bytes=56 << 20),
-        cost_estimate=cost(part / 200),
+        cost_estimate=cost(20),
         name="project",
-    )(*operands)
+    )(offsets, rows, weight, *terms)
 
 
 def spread(held, digit):
@@ -212,11 +203,7 @@
 def shards(pops, tps, tokens, norm_gain, weight, pair_seeds, member_ranks):
     owned_rows, width = weight.shape
     pop_index, tp_index = lax.axis_index("pop"), lax.axis_index("tp")
-    split = width * 4 // 5 // 128 * 128
-    gathered = [
-        lax.all_gather(weight[:, :split], "pop", axis=0, tiled=True),
-        lax.all_gather(weight[:, split:], "pop", axis=0, tiled=True),
-    ]
+    gathered = lax.all_gather(weight, "pop", axis=0, tiled=True)
     pairs = pair_seeds.shape[0]
     col_start = tp_index * width
     starts = pair_seeds * jnp.int32(mix_seed) + col_start
@@ -255,10 +242,7 @@
     offsets = jnp.stack([place * span for place in order]).astype(jnp.int32)
     normed = jnp.concatenate(pieces, 0)
     terms, estimate = lax.optimization_barrier((terms, estimate))
-    activated, first = None, 0
-    for piece in gathered:
-        activated = project(offsets, normed, piece, terms, activated, first, width)
-        first += piece.shape[1]
+    activated = project(offsets, normed, gathered, terms)
     return (activated, estimate)
 
 

time: 247 us -> 226 us (0.915)
  waiting for transfers between devices: 21.8 us -> 8.75 us
  Pallas kernels: 188 us -> 183 us
  local copies, waits for them, and re-layouts: 6.49 us -> 1.69 us
    all_gather x2 -> x1, waiting for transfers between devices: 21.7 us -> 8.06 us  [shards(): gathered = lax.all_gather(weight, 'pop', axis=0, tiled=True)]
    pallas_call x2 -> x1, Pallas kernels: 29 us -> 23.2 us  [project(): pl.pallas_call(functools.partial(project_kernel, len(terms)), out_shape=j...]
    slice x2 -> x0, local copies, waits for them, and re-layouts: 4.86 us -> none  [the longest x1 3.02 us: shards(): weight[:, :split]]
  transfers between devices with their start and end apart: 9 -> 8, of which waited for: 1 -> 1; matrix products, arithmetic and copies ran while one was open for 4% -> 5% of each run, Pallas kernels for 73% -> 71%
where the time goes in v3:
time: 226 us; the launch traced here: 225 us
  Pallas kernels  183 us (81%)
  between operations  14.1 us (6%)
  starting transfers between devices  9.32 us (4%)
  other arithmetic  8.79 us (4%)
  waiting for transfers between devices  8.75 us (4%)
    pallas_call x2, Pallas kernels, noise_term(): pl.pallas_call(functools.partial(term_kernel, tile), out_shape=jax.ShapeD...  82.5 us
    pallas_call x1, Pallas kernels, make_estimate(): pl.pallas_call(functools.partial(estimate_kernel, tile, 128 * (members -...  77.1 us
    pallas_call x1, Pallas kernels, project(): pl.pallas_call(functools.partial(project_kernel, len(terms)), out_shape=j...  23.2 us
    all_gather x1, waiting for transfers between devices, shards(): gathered = lax.all_gather(weight, 'pop', axis=0, tiled=True)  8.06 us
    ppermute x6, starting transfers between devices, collect(): lax.ppermute(block, axis, [(i, i ^ k * step) for i in range(size)])  7.51 us
  transfers between devices with their start and end apart: 8, of which 1 were waited for; matrix products, arithmetic and copies ran while one was open for 5% of the time, Pallas kernels for 71%

profile of v3, /device:TPU:0, one launch (start us, length us, event | category | flops | bytes accessed | tf_op | source)
XLA Modules:
  0.0 225.4 jit_solution(8273785800400563993)
XLA Ops:
  7.2 0.7 all-gather.2.cloned.1.call-update
  7.9 0.7 add_bitcast_fusion
  8.7 2.4 %collective-permute-start.3 = (s32[1,6]{1,0:T(1,128)S(1)}, s32[1,6]{1,0:T(1,128)S(1)}, u32[]{:S(2)}, u32[]{:S(2)}) collective-permute-start(s32[1,6]{1,0:T(1,128)S(1)} %add_bitcast_fusion), channel_id=1, source_target_pairs={{0,6},{2,4},{4,2},{6,0},{8,14},{10,12},{12,10},{14,8},{16,22},{18,... | collective-permute-start | bytes 80 | tf_op jit(solution)/shard_map/ppermute | solution.py:192
  11.0 0.6 collective-permute-start.2
  11.7 1.8 collective-permute-start
  13.5 0.7 convert_element_type.17
  14.2 0.7 multiply_add_fusion
  14.8 0.7 fusion.6
  15.5 0.4 fusion
  15.9 1.5 fusion.2.rows_ref
  17.4 41.3 %noise_term.2.refs_0_ = f32[192,5120]{1,0:T(8,128)} custom-call(s32[1]{0:T(128)} %get-tuple-element.47.start_ref, bf16[192,3584]{1,0:T(8,128)(2,1)} %fusion.2.rows_ref), custom_call_target="tpu_custom_call" | custom-call | flops 41999998976 | bytes 1048576 | tf_op jit(solution)/shard_map/noise_term/pallas_call | solution.py:82
  58.7 0.6 pad_add_fusion.2.offsets_ref
  59.3 3.6 %collective-permute-start.6 = (s32[4,6]{1,0:T(4,128)S(1)}, s32[4,6]{1,0:T(4,128)S(1)}, u32[]{:S(2)}, u32[]{:S(2)}) collective-permute-start(s32[4,6]{1,0:T(4,128)S(1)} %pad_add_fusion.1), channel_id=1, source_target_pairs={{0,24},{2,26},{4,28},{6,30},{8,16},{10,18},{12,20},{14,22},{16,8},... | collective-permute-start | bytes 296 | tf_op jit(solution)/shard_map/ppermute | solution.py:192
  62.9 0.8 collective-permute-start.4
  63.8 0.4 fusion.3
  64.2 1.5 fusion.5.rows_ref
  65.6 41.1 %noise_term.3.refs_1_ = f32[192,5120]{1,0:T(8,128)} custom-call(s32[1]{0:T(128)} %get-tuple-element.46.start_ref, bf16[192,3584]{1,0:T(8,128)(2,1)} %fusion.5.rows_ref), custom_call_target="tpu_custom_call" | custom-call | flops 41999998976 | bytes 1048576 | tf_op jit(solution)/shard_map/noise_term/pallas_call | solution.py:82
  106.8 1.8 pad_maximum_fusion.rows_ref
  108.8 0.1 slice.15
  109.1 0.6 add.76.starts_ref
  109.7 0.5 sub.9.ranks_ref
  110.2 77.1 %estimate.1 = f32[224,5120]{1,0:T(8,128)} custom-call(s32[32]{0:T(128)} %add.76.starts_ref, s32[32]{0:T(128)} %sub.9.ranks_ref), custom_call_target="tpu_custom_call" | custom-call | flops 74999996416 | bytes 1048576 | tf_op jit(solution)/shard_map/estimate/pallas_call | solution.py:126
  187.3 8.1 %all-gather.2.cloned.1.call-done.weight_ref = bf16[3584,5120]{1,0:T(8,128)(2,1)} async-done(((bf16[224,5120]{1,0:T(8,128)(2,1)}), bf16[3584,5120]{1,0:T(8,128)(2,1)}) %all-gather.2.cloned.1.call-update) | async-done | bytes 36700176 | tf_op jit(solution)/shard_map/all_gather | solution.py:206
  195.4 23.2 %project.1 = bf16[384,5120]{1,0:T(8,128)(2,1)} custom-call(s32[2]{0:T(128)} %pad_add_fusion.2.offsets_ref, bf16[384,3584]{1,0:T(8,128)(2,1)} %pad_maximum_fusion.rows_ref, bf16[3584,5120]{1,0:T(8,128)(2,1)} %all-gather.2.cloned.1.call-done.weight_ref, f32[192,5120]{1,0:T(8,128)} %noise_term.2.refs_0_, f32[192,5120]{1,0:T(8,128)} %noise_term.3.refs_1_), custom_call_target="tpu_custom_call" | custom-call | flops 20000000000 | bytes 1048576 | tf_op jit(solution)/shard_map/project/pallas_call | solution.py:158
  (26 shorter events, 0.5 us)
Async XLA Ops:
  7.2 8.3 %copy-start = (bf16[192,3584]{1,0:T(8,128)(2,1)S(1)}, bf16[192,3584]{1,0:T(8,128)(2,1)}, u32[]{:S(2)}) copy-start(bf16[192,3584]{1,0:T(8,128)(2,1)} %param.5) | copy-start | bytes 4128772
  7.2 188.2 %all-gather.2.cloned.1.call-start = ((), (), s32[]{:S(2)}) async-start(), calls=%async_computation | async-start | bytes 38993920 | tf_op jit(solution)/shard_map/all_gather | solution.py:206
  8.7 50.6 %collective-permute-start.3 = (s32[1,6]{1,0:T(1,128)S(1)}, s32[1,6]{1,0:T(1,128)S(1)}, u32[]{:S(2)}, u32[]{:S(2)}) collective-permute-start(s32[1,6]{1,0:T(1,128)S(1)} %add_bitcast_fusion), channel_id=1, source_target_pairs={{0,6},{2,4},{4,2},{6,0},{8,14},{10,12},{12,10},{14,8},{16,22},{18,... | collective-permute-start | bytes 80 | tf_op jit(solution)/shard_map/ppermute | solution.py:192
  11.0 48.3 %collective-permute-start.2 = (s32[1,6]{1,0:T(1,128)S(1)}, s32[1,6]{1,0:T(1,128)S(1)}, u32[]{:S(2)}, u32[]{:S(2)}) collective-permute-start(s32[1,6]{1,0:T(1,128)S(1)} %add_bitcast_fusion), channel_id=1, source_target_pairs={{0,4},{2,6},{4,0},{6,2},{8,12},{10,14},{12,8},{14,10},{16,20},{18,... | collective-permute-start | bytes 80 | tf_op jit(solution)/shard_map/ppermute | solution.py:192
  11.7 47.6 %collective-permute-start.1 = (s32[1,6]{1,0:T(1,128)S(1)}, s32[1,6]{1,0:T(1,128)S(1)}, u32[]{:S(2)}, u32[]{:S(2)}) collective-permute-start(s32[1,6]{1,0:T(1,128)S(1)} %add_bitcast_fusion), channel_id=1, source_target_pairs={{0,2},{2,0},{4,6},{6,4},{8,10},{10,8},{12,14},{14,12},{16,18},{18,... | collective-permute-start | bytes 80 | tf_op jit(solution)/shard_map/ppermute | solution.py:192
  11.7 47.6 %collective-permute-start = (bf16[192,3584]{1,0:T(8,128)(2,1)}, bf16[192,3584]{1,0:T(8,128)(2,1)S(1)}, u32[]{:S(2)}, u32[]{:S(2)}) collective-permute-start(bf16[192,3584]{1,0:T(8,128)(2,1)} %param.5), channel_id=1, source_target_pairs={{1,0},{0,1},{3,2},{2,3},{5,4},{4,5},{7,6},{6,7},{9,8},{8,9},{11,10... | collective-permute-start | bytes 4128776 | tf_op jit(solution)/shard_map/ppermute | solution.py:215
  59.3 49.3 %collective-permute-start.6 = (s32[4,6]{1,0:T(4,128)S(1)}, s32[4,6]{1,0:T(4,128)S(1)}, u32[]{:S(2)}, u32[]{:S(2)}) collective-permute-start(s32[4,6]{1,0:T(4,128)S(1)} %pad_add_fusion.1), channel_id=1, source_target_pairs={{0,24},{2,26},{4,28},{6,30},{8,16},{10,18},{12,20},{14,22},{16,8},... | collective-permute-start | bytes 296 | tf_op jit(solution)/shard_map/ppermute | solution.py:192
  62.9 45.7 %collective-permute-start.5 = (s32[4,6]{1,0:T(4,128)S(1)}, s32[4,6]{1,0:T(4,128)S(1)}, u32[]{:S(2)}, u32[]{:S(2)}) collective-permute-start(s32[4,6]{1,0:T(4,128)S(1)} %pad_add_fusion.1), channel_id=1, source_target_pairs={{0,16},{2,18},{4,20},{6,22},{8,24},{10,26},{12,28},{14,30},{16,0},... | collective-permute-start | bytes 296 | tf_op jit(solution)/shard_map/ppermute | solution.py:192
  62.9 45.7 %collective-permute-start.4 = (s32[4,6]{1,0:T(4,128)S(1)}, s32[4,6]{1,0:T(4,128)S(1)}, u32[]{:S(2)}, u32[]{:S(2)}) collective-permute-start(s32[4,6]{1,0:T(4,128)S(1)} %pad_add_fusion.1), channel_id=1, source_target_pairs={{0,8},{2,10},{4,12},{6,14},{8,0},{10,2},{12,4},{14,6},{16,24},{18,... | collective-permute-start | bytes 296 | tf_op jit(solution)/shard_map/ppermute | solution.py:192
  65.6 41.2 %copy-start.1 = (bf16[192,3584]{1,0:T(8,128)(2,1)S(1)}, bf16[192,3584]{1,0:T(8,128)(2,1)}, u32[]{:S(2)}) copy-start(bf16[192,3584]{1,0:T(8,128)(2,1)} %fusion.2.rows_ref) | copy-start | bytes 4128772
  65.6 41.2 %copy-start.2 = (bf16[192,3584]{1,0:T(8,128)(2,1)S(1)}, bf16[192,3584]{1,0:T(8,128)(2,1)}, u32[]{:S(2)}) copy-start(bf16[192,3584]{1,0:T(8,128)(2,1)} %fusion.5.rows_ref) | copy-start | bytes 4128772
Sparse Core Ops, SparseCore 0:
  9.6 185.6 all-gather.1
